TPU v7x, 256 devices: a whole 4x4x8 slice. The times are simulated.
256 devices in a mesh: table: 16 (over y_lo, x, core), tensor: 2 (over y_hi), dp: 8 (over z).
Axes of the slice: x: 4, y: 4 (y_hi: 2, y_lo: 2; y = y_hi * 2 + y_lo), z: 8, core: 2. Of those that a mesh axis runs over, the one named last changes fastest.
Arguments:
- lookup_ids: int32 [4096, 16, 16], P('dp', 'table'), may hold values from 0 to 4095
- bag_lengths: int32 [4096, 16], P('dp', 'table'), may hold values from 1 to 16
- feature_widths: int32 [16], replicated, may hold values from 32 to 256, as said below
- tables: bfloat16 [16, 4096, 256], P('table', None, 'tensor'), may hold values from -6 to 6
- w_in: bfloat16 [4096, 16384], P(None, ('table', 'tensor')), may hold values from -0.25 to 0.25
- w_out: bfloat16 [16384, 4096], P(('table', 'tensor')), may hold values from -0.1875 to 0.1875
- cotangent: bfloat16 [4096, 4096], P('dp', ('table', 'tensor')), may hold values from -6 to 6
Outputs:
- mixed_out: bfloat16 [4096, 4096], P('dp', ('table', 'tensor'))
- grad_in: float32 [4096, 16384], P('dp', ('table', 'tensor'))
- grad_out: float32 [16384, 4096], P(('table', 'tensor', 'dp'))
Inputs may be any that keep to these rules, and one draw needn't show every extreme that they name: `feature_widths`: multiples of 32; one feature has exactly 256, another exactly 32.
All inputs are finite; a program needn't handle non-finite values.
Results may differ from a plain program's by a relative error of at most 0.0056.
Values may be sent and summed in bfloat16 or wider, within the bound.
A program may use at most 128 MiB of HBM per device.

v0:
```python
import jax
import jax.numpy as jnp
from jax import lax
from jax.sharding import PartitionSpec as P


def silu_slope(preact):
    sigmoid_part = jax.nn.sigmoid(preact)
    return sigmoid_part * (1.0 + preact * (1.0 - sigmoid_part))


def pool_local(lookup, lengths, embedding):
    samples, bag_size = lookup.shape
    vocab, half_width = embedding.shape
    vocab_block = min(vocab, 512)
    in_bag = jnp.arange(bag_size)[None, :] < lengths[:, None]
    masked = jnp.where(in_bag, lookup, -1)

    def add_block(running, first_row):
        local_ids = first_row + jnp.arange(vocab_block)
        counts = jnp.sum(masked[:, :, None] == local_ids[None, None, :], axis=1).astype(
            jnp.bfloat16
        )
        table_rows = lax.dynamic_slice_in_dim(embedding, first_row, vocab_block, 0)
        return (running + jnp.dot(counts, table_rows, preferred_element_type=jnp.float32), None)

    starts = jnp.arange(vocab // vocab_block) * vocab_block
    summed, unused = lax.scan(add_block, jnp.zeros((samples, half_width), jnp.float32), starts)
    return summed / lengths[:, None].astype(jnp.float32)


def shards(lookup_ids, bag_lengths, feature_widths, tables, w_in, w_out, cotangent):
    embedding = tables[0]
    half_width = embedding.shape[1]
    summed = pool_local(lookup_ids[:, 0, :], bag_lengths[:, 0], embedding)
    own_width = lax.dynamic_index_in_dim(feature_widths, lax.axis_index("table"), 0, keepdims=False)
    positions = lax.axis_index("tensor") * half_width + jnp.arange(half_width)
    pooled = jnp.where(positions[None, :] < own_width, summed, jnp.zeros_like(summed)).astype(
        jnp.bfloat16
    )
    features = lax.all_gather(pooled, ("table", "tensor"), axis=1, tiled=True)
    preact = jnp.dot(features, w_in, preferred_element_type=jnp.float32)
    hidden = jax.nn.silu(preact).astype(jnp.bfloat16)
    partial_out = jnp.dot(hidden, w_out, preferred_element_type=jnp.float32)
    reduced = lax.psum_scatter(partial_out, ("table", "tensor"), scatter_dimension=1, tiled=True)
    mixed_out = reduced.astype(jnp.bfloat16)
    whole_grad = lax.all_gather(cotangent, ("table", "tensor"), axis=1, tiled=True)
    contract_rows = (((0,), (0,)), ((), ()))
    contract_cols = (((1,), (1,)), ((), ()))
    grad_hidden = lax.dot_general(
        whole_grad, w_out, contract_cols, preferred_element_type=jnp.float32
    )
    grad_preact = (grad_hidden * silu_slope(preact)).astype(jnp.bfloat16)
    term_in = lax.dot_general(
        features, grad_preact, contract_rows, preferred_element_type=jnp.float32
    )
    term_out = lax.dot_general(
        hidden, whole_grad, contract_rows, preferred_element_type=jnp.float32
    )
    grad_in, grad_out = (
        lax.psum_scatter(term_in, "dp", scatter_dimension=0, tiled=True),
        lax.psum_scatter(term_out, "dp", scatter_dimension=0, tiled=True),
    )
    return (mixed_out, grad_in, grad_out)


def solution(mesh):
    return jax.shard_map(
        shards,
        mesh=mesh,
        in_specs=(
            P("dp", "table", None),
            P("dp", "table"),
            P(),
            P("table", None, "tensor"),
            P(None, ("table", "tensor")),
            P(("table", "tensor"), None),
            P("dp", ("table", "tensor")),
        ),
        out_specs=(
            P("dp", ("table", "tensor")),
            P("dp", ("table", "tensor")),
            P(("table", "tensor", "dp"), None),
        ),
        check_vma=False,
    )
```

profile of v0, /device:TPU:1, one launch (start us, length us, event | category | flops | bytes accessed | tf_op | source)
XLA Modules:
  0.0 646.2 jit_solution(7221660511315152307)
XLA Ops:
  7.2 0.7 convert_element_type.21
  7.9 0.9 copy.11
  8.8 0.8 bitcast_select_fusion
  9.6 64.7 %while.11 = (s32[]{:T(128)}, f32[512,128]{1,0:T(8,128)S(1)}, s32[512,16]{1,0:T(8,128)S(1)}, s32[8]{0:T(128)S(1)}, bf16[4096,128]{1,0:T(8,128)(2,1)}, /*index=5*/s32[]{:T(128)}, s32[]{:T(128)}, s32[]{:T(128)}) while((s32[]{:T(128)}, f32[512,128]{1,0:T(8,128)S(1)}, s32[512,16]{1,0:T(8,128)S(1)}, s32[8]{0:T(128)S(1)}, ...), condition=%wide.region_2.3_spmd.clone, body=%wide.region_0.2_spmd.clone.sunk | while | flops 79823368 | bytes 2789533 | solution.py:28
  9.7 0.6 dynamic_slice.19
  12.2 0.6 iota_add_fusion.2
  12.8 3.6 convert_reduce_fusion.2
  16.5 1.2 convolution_add_fusion.2
  17.8 0.6 dynamic_slice.19
  20.3 0.6 iota_add_fusion.2
  20.9 3.6 convert_reduce_fusion.2
  24.6 1.2 convolution_add_fusion.2
  25.8 0.6 dynamic_slice.19
  28.4 0.6 iota_add_fusion.2
  29.0 3.6 convert_reduce_fusion.2
  32.7 1.2 convolution_add_fusion.2
  33.9 0.6 dynamic_slice.19
  36.5 0.6 iota_add_fusion.2
  37.1 3.6 convert_reduce_fusion.2
  40.7 1.2 convolution_add_fusion.2
  42.0 0.6 dynamic_slice.19
  44.5 0.6 iota_add_fusion.2
  45.2 3.6 convert_reduce_fusion.2
  48.8 1.2 convolution_add_fusion.2
  52.6 0.6 iota_add_fusion.2
  53.3 3.6 convert_reduce_fusion.2
  56.9 1.2 convolution_add_fusion.2
  60.7 0.6 iota_add_fusion.2
  61.4 3.6 convert_reduce_fusion.2
  65.0 1.2 convolution_add_fusion.2
  68.8 0.6 iota_add_fusion.2
  69.5 3.6 convert_reduce_fusion.2
  73.1 1.2 convolution_add_fusion.2
  74.4 0.6 dynamic_slice.11
  75.0 0.7 add_compare_fusion
  75.6 0.8 select_convert_fusion
  76.5 0.7 all-gather.5.cloned.1.call-update
  77.2 89.7 %all-gather.3.cloned.1.call-done = bf16[512,4096]{1,0:T(8,128)(2,1)} async-done(((bf16[512,128]{1,0:T(8,128)(2,1)}), bf16[512,4096]{1,0:T(8,128)(2,1)}) %all-gather.3.cloned.1.call-update) | async-done | bytes 4194320 | tf_op jit(solution)/shard_map/all_gather | solution.py:41
  166.9 5.9 fusion.6
  172.8 5.6 fusion.5
  178.5 74.9 %all-gather.5.cloned.1.call-done = bf16[512,4096]{1,0:T(8,128)(2,1)} async-done(((bf16[512,128]{1,0:T(8,128)(2,1)}), bf16[512,4096]{1,0:T(8,128)(2,1)}) %all-gather.5.cloned.1.call-update) | async-done | bytes 4194320 | tf_op jit(solution)/shard_map/all_gather | solution.py:47
  253.4 6.1 fusion.3
  259.6 5.7 fusion.7
  265.3 7.9 %fusion.4 = f32[512,4096]{1,0:T(8,128)} fusion(bf16[512,4096]{1,0:T(8,128)(2,1)} %all-gather.5.cloned.1.call-done, f32[512,512]{1,0:T(8,128)S(1)} %fusion.6), kind=kOutput, calls=%fused_computation.15 | convolution fusion | flops 2148794368 | bytes 13631488 | tf_op jit(solution)/shard_map/dot_general | solution.py:57
  273.2 170.3 %reduce-scatter.4.cloned.1.call-done = f32[512,128]{1,0:T(8,128)} async-done(((f32[512,4096]{1,0:T(8,128)}), f32[512,128]{1,0:T(8,128)}) %reduce-scatter.4.cloned.1.call-update) | async-done | bytes 262160 | tf_op jit(solution)/shard_map/reduce_scatter | solution.py:45
  443.6 1.6 convert_element_type.24
  445.2 97.9 %reduce-scatter.6.cloned.1.call-done = f32[512,512]{1,0:T(8,128)} async-done(((f32[4096,512]{1,0:T(8,128)}), f32[512,512]{1,0:T(8,128)}) %reduce-scatter.6.cloned.1.call-update) | async-done | bytes 1048592 | tf_op jit(solution)/shard_map/reduce_scatter | solution.py:61
  543.1 96.6 %reduce-scatter.8.cloned.1.call-done = f32[64,4096]{1,0:T(8,128)} async-done(((f32[512,4096]{1,0:T(8,128)}), f32[64,4096]{1,0:T(8,128)}) %reduce-scatter.8.cloned.1.call-update) | async-done | bytes 1048592 | tf_op jit(solution)/shard_map/reduce_scatter | solution.py:62
  (20 shorter events, 2.0 us)
Async XLA Ops:
  7.2 159.7 %all-gather.3.cloned.1.call-start = ((), (), s32[]{:S(2)}) async-start(), calls=%async_computation.3 | async-start | bytes 4325376 | tf_op jit(solution)/shard_map/all_gather | solution.py:41
  9.6 64.7 %copy-start.2 = (s32[16]{0:T(128)S(1)}, s32[16]{0:T(128)}, u32[]{:S(2)}) copy-start(s32[16]{0:T(128)} %param.11) | copy-start | bytes 196
  76.4 177.0 %all-gather.5.cloned.1.call-start = ((), (), s32[]{:S(2)}) async-start(), calls=%async_computation.5 | async-start | bytes 4325376 | tf_op jit(solution)/shard_map/all_gather | solution.py:47
  77.2 366.4 %reduce-scatter.4.cloned.1.call-start = ((), (), s32[]{:S(2)}) async-start(), calls=%async_computation.4 | async-start | bytes 8650752 | tf_op jit(solution)/shard_map/reduce_scatter | solution.py:45
  166.9 5.9 copy-start.1
  178.5 364.6 %reduce-scatter.6.cloned.1.call-start = ((), (), s32[]{:S(2)}) async-start(), calls=%async_computation.6 | async-start | bytes 9437184 | tf_op jit(solution)/shard_map/reduce_scatter | solution.py:61
  253.4 6.1 copy-start
  265.3 374.5 %reduce-scatter.8.cloned.1.call-start = ((), (), s32[]{:S(2)}) async-start(), calls=%async_computation.7 | async-start | bytes 9437184 | tf_op jit(solution)/shard_map/reduce_scatter | solution.py:62
Sparse Core Ops, SparseCore 0:
  76.6 90.2 all-gather.2
  168.6 84.7 all-gather.4
  256.0 187.5 reduce-scatter.3
  446.5 96.5 reduce-scatter.5
  546.1 93.5 reduce-scatter.7
where the time goes:
time: 647 us; the launch traced here: 646 us
  waiting for transfers between devices  530 us (82%)
  matrix products  41.2 us (6%)
  other arithmetic  38.8 us (6%)
  loops' own time  15.9 us (2%)
  between operations  13.9 us (2%)
    reduce_scatter x1, waiting for transfers between devices, shards(): lax.psum_scatter(partial_out, ('table', 'tensor'), scatter_dimension=1, t...  170 us
    reduce_scatter x1, waiting for transfers between devices, shards(): lax.psum_scatter(term_in, 'dp', scatter_dimension=0, tiled=True)  97.9 us
    reduce_scatter x1, waiting for transfers between devices, shards(): lax.psum_scatter(term_out, 'dp', scatter_dimension=0, tiled=True)  96.6 us
    all_gather x1, waiting for transfers between devices, shards(): features = lax.all_gather(pooled, ('table', 'tensor'), axis=1, tiled=True)  89.7 us
    all_gather x1, waiting for transfers between devices, shards(): lax.all_gather(cotangent, ('table', 'tensor'), axis=1, tiled=True)  74.9 us
    reduce_sum x8, other arithmetic, add_block(): jnp.sum(masked[:, :, None] == local_ids[None, None, :], axis=1)  29 us
    another operation x1, loops' own time, pool_local(): lax.scan(add_block, jnp.zeros((samples, half_width), jnp.float32), starts)  15.9 us
  transfers between devices with their start and end apart: 5, of which 5 were waited for; matrix products, arithmetic and copies ran while one was open for 5% of the time, Pallas kernels for 0%

commit v1 on v0

--- a/solution.py
+++ b/solution.py
@@ -38,7 +38,12 @@
     pooled = jnp.where(positions[None, :] < own_width, summed, jnp.zeros_like(summed)).astype(
         jnp.bfloat16
     )
-    features = lax.all_gather(pooled, ("table", "tensor"), axis=1, tiled=True)
+    features = jnp.concatenate(
+        lax.all_to_all(
+            jnp.stack([pooled] * lax.axis_size(("table", "tensor"))), ("table", "tensor"), 0, 0
+        ),
+        axis=1,
+    )
     preact = jnp.dot(features, w_in, preferred_element_type=jnp.float32)
     hidden = jax.nn.silu(preact).astype(jnp.bfloat16)
     partial_out = jnp.dot(hidden, w_out, preferred_element_type=jnp.float32)

time: 647 us -> 541 us (0.84)
  waiting for transfers between devices: 530 us -> 366 us
  blocking collectives: 0 us -> 61.2 us
    all_gather x1 -> x0, waiting for transfers between devices: 89.7 us -> none  [shards(): features = lax.all_gather(pooled, ('table', 'tensor'), axis=1, tiled=True)]
    all_gather x1, waiting for transfers between devices: 74.9 us -> 0.02 us  [shards(): lax.all_gather(cotangent, ('table', 'tensor'), axis=1, tiled=True)]
    all_to_all x0 -> x1, blocking collectives: none -> 61.2 us  [shards(): lax.all_to_all(jnp.stack([pooled] * lax.axis_size(('table', 'tensor'))),...]
  transfers between devices with their start and end apart: 5 -> 4, of which waited for: 5 -> 3; matrix products, arithmetic and copies ran while one was open for 5% -> 15% of each run, Pallas kernels for 0% -> 0%
where the time goes in v1:
time: 541 us
  waiting for transfers between devices  366 us (68%)
  blocking collectives  61.2 us (11%)
  matrix products  37.6 us (7%)
  other arithmetic  37.4 us (7%)
  loops' own time  15.9 us (3%)
  between operations  13.9 us (3%)
  local copies, waits for them, and re-layouts  8.72 us (2%)
    reduce_scatter x1, waiting for transfers between devices, shards(): lax.psum_scatter(partial_out, ('table', 'tensor'), scatter_dimension=1, t...  170 us
    reduce_scatter x1, waiting for transfers between devices, shards(): lax.psum_scatter(term_in, 'dp', scatter_dimension=0, tiled=True)  98.2 us
    reduce_scatter x1, waiting for transfers between devices, shards(): lax.psum_scatter(term_out, 'dp', scatter_dimension=0, tiled=True)  96.6 us
    all_to_all x1, blocking collectives, shards(): lax.all_to_all(jnp.stack([pooled] * lax.axis_size(('table', 'tensor'))),...  61.2 us
    reduce_sum x8, other arithmetic, add_block(): jnp.sum(masked[:, :, None] == local_ids[None, None, :], axis=1)  29 us
    another operation x1, loops' own time, pool_local(): lax.scan(add_block, jnp.zeros((samples, half_width), jnp.float32), starts)  15.9 us
  transfers between devices with their start and end apart: 4, of which 3 were waited for; matrix products, arithmetic and copies ran while one was open for 15% of the time, Pallas kernels for 0%

profile of v1, /device:TPU:1, one launch (start us, length us, event | category | flops | bytes accessed | tf_op | source)
XLA Modules:
  0.0 540.7 jit_solution(6568333351670892574)
XLA Ops:
  7.2 0.7 all-gather.2.cloned.1.call-update
  8.0 0.9 copy.13
  8.9 0.8 bitcast_select_fusion
  9.7 64.7 %while.11 = (s32[]{:T(128)}, f32[512,128]{1,0:T(8,128)S(1)}, s32[512,16]{1,0:T(8,128)S(1)}, s32[8]{0:T(128)S(1)}, bf16[4096,128]{1,0:T(8,128)(2,1)}, /*index=5*/s32[]{:T(128)}, s32[]{:T(128)}, s32[]{:T(128)}) while((s32[]{:T(128)}, f32[512,128]{1,0:T(8,128)S(1)}, s32[512,16]{1,0:T(8,128)S(1)}, s32[8]{0:T(128)S(1)}, ...), condition=%wide.region_2.3_spmd.clone, body=%wide.region_0.2_spmd.clone.sunk | while | flops 79823368 | bytes 2789533 | solution.py:28
  12.2 0.6 iota_add_fusion.2
  12.9 3.6 convert_reduce_fusion.2
  16.5 1.2 convolution_add_fusion.2
  17.8 0.6 dynamic_slice.19
  20.3 0.6 iota_add_fusion.2
  21.0 3.6 convert_reduce_fusion.2
  24.6 1.2 convolution_add_fusion.2
  25.9 0.6 dynamic_slice.19
  28.4 0.6 iota_add_fusion.2
  29.1 3.6 convert_reduce_fusion.2
  32.7 1.2 convolution_add_fusion.2
  34.0 0.6 dynamic_slice.19
  36.5 0.6 iota_add_fusion.2
  37.2 3.6 convert_reduce_fusion.2
  40.8 1.2 convolution_add_fusion.2
  42.1 0.6 dynamic_slice.19
  44.6 0.6 iota_add_fusion.2
  45.3 3.6 convert_reduce_fusion.2
  48.9 1.2 convolution_add_fusion.2
  50.2 0.6 dynamic_slice.19
  52.7 0.7 iota_add_fusion.2
  53.4 3.6 convert_reduce_fusion.2
  57.0 1.2 convolution_add_fusion.2
  58.2 0.6 dynamic_slice.19
  60.8 0.6 iota_add_fusion.2
  61.4 3.6 convert_reduce_fusion.2
  65.1 1.2 convolution_add_fusion.2
  66.3 0.6 dynamic_slice.19
  68.9 0.6 iota_add_fusion.2
  69.5 3.6 convert_reduce_fusion.2
  73.2 1.2 convolution_add_fusion.2
  74.5 0.6 dynamic_slice.11
  75.0 0.7 add_compare_fusion
  76.5 61.2 %all_to_all.5 = bf16[32,512,128]{1,2,0:T(8,128)(2,1)S(1)} all-to-all(bf16[32,512,128]{1,2,0:T(8,128)(2,1)S(1)} %stack.2), channel_id=1, replica_groups=mesh['table'=16,'tensor'=2,'dp'=8] {'table','tensor'}, dimensions={0} | all-to-all | bytes 8388608 | tf_op jit(solution)/shard_map/all_to_all | solution.py:42
  137.7 2.0 copy-done
  139.6 2.3 fusion.6
  142.0 5.6 %fusion.5 = f32[512,4096]{1,0:T(8,128)} fusion(bf16[512,4096]{1,0:T(8,128)(2,1)S(1)} %copy-done.3, f32[512,512]{1,0:T(8,128)S(1)} %fusion.6), kind=kOutput, calls=%fused_computation.16 | convolution fusion | flops 2148794368 | bytes 13631488 | tf_op jit(solution)/shard_map/dot_general | solution.py:49
  147.7 6.1 %fusion.3 = bf16[512,512]{1,0:T(8,128)(2,1)S(1)} fusion(bf16[512,4096]{1,0:T(8,128)(2,1)} %all-gather.2.cloned.1.call-done, bf16[512,4096]{1,0:T(8,128)(2,1)} %param.14, f32[512,512]{1,0:T(8,128)S(1)} %fusion.6), kind=kOutput, calls=%fused_computation.7 | convolution fusion | flops 2149842944 | bytes 9961472 | tf_op jit(solution)/shard_map/dot_general | solution.py:55
  153.9 5.7 %fusion.7 = f32[4096,512]{1,0:T(8,128)} fusion(bf16[512,4096]{0,1:T(8,128)(2,1)S(1)} %bitcast.21, bf16[512,512]{1,0:T(8,128)(2,1)S(1)} %fusion.3), kind=kOutput, calls=%fused_computation.18 | convolution fusion | flops 2147483648 | bytes 13107200 | tf_op jit(solution)/shard_map/dot_general | solution.py:59
  159.6 7.9 %fusion.4 = f32[512,4096]{1,0:T(8,128)} fusion(bf16[512,4096]{1,0:T(8,128)(2,1)} %all-gather.2.cloned.1.call-done, f32[512,512]{1,0:T(8,128)S(1)} %fusion.6), kind=kOutput, calls=%fused_computation.15 | convolution fusion | flops 2148794368 | bytes 13631488 | tf_op jit(solution)/shard_map/dot_general | solution.py:62
  167.5 170.3 %reduce-scatter.4.cloned.1.call-done = f32[512,128]{1,0:T(8,128)} async-done(((f32[512,4096]{1,0:T(8,128)}), f32[512,128]{1,0:T(8,128)}) %reduce-scatter.4.cloned.1.call-update) | async-done | bytes 262160 | tf_op jit(solution)/shard_map/reduce_scatter | solution.py:50
  337.8 1.6 convert_element_type.24
  339.4 98.2 %reduce-scatter.6.cloned.1.call-done = f32[512,512]{1,0:T(8,128)} async-done(((f32[4096,512]{1,0:T(8,128)}), f32[512,512]{1,0:T(8,128)}) %reduce-scatter.6.cloned.1.call-update) | async-done | bytes 1048592 | tf_op jit(solution)/shard_map/reduce_scatter | solution.py:66
  437.6 96.6 %reduce-scatter.8.cloned.1.call-done = f32[64,4096]{1,0:T(8,128)} async-done(((f32[512,4096]{1,0:T(8,128)}), f32[64,4096]{1,0:T(8,128)}) %reduce-scatter.8.cloned.1.call-update) | async-done | bytes 1048592 | tf_op jit(solution)/shard_map/reduce_scatter | solution.py:67
  (26 shorter events, 1.6 us)
Async XLA Ops:
  7.2 140.6 %all-gather.2.cloned.1.call-start = ((), (), s32[]{:S(2)}) async-start(), calls=%async_computation.5 | async-start | bytes 4325376 | tf_op jit(solution)/shard_map/all_gather | solution.py:52
  7.9 329.9 %reduce-scatter.4.cloned.1.call-start = ((), (), s32[]{:S(2)}) async-start(), calls=%async_computation.4 | async-start | bytes 8650752 | tf_op jit(solution)/shard_map/reduce_scatter | solution.py:50
  9.7 64.7 %copy-start.4 = (s32[512,1]{0,1:T(1,128)S(1)}, s32[512,1]{0,1:T(1,128)}, u32[]{:S(2)}) copy-start(s32[512,1]{0,1:T(1,128)} %param.10) | copy-start | bytes 6148
  9.7 64.8 %copy-start.5 = (s32[16]{0:T(128)S(1)}, s32[16]{0:T(128)}, u32[]{:S(2)}) copy-start(s32[16]{0:T(128)} %param.11) | copy-start | bytes 196
  76.4 63.2 %copy-start.2 = (bf16[4096,512]{1,0:T(8,128)(2,1)S(1)}, bf16[4096,512]{1,0:T(8,128)(2,1)}, u32[]{:S(2)}) copy-start(bf16[4096,512]{1,0:T(8,128)(2,1)} %param.13) | copy-start | bytes 12582916
  137.7 2.0 copy-start
  139.6 2.4 copy-start.3
  147.6 289.9 %reduce-scatter.6.cloned.1.call-start = ((), (), s32[]{:S(2)}) async-start(), calls=%async_computation.6 | async-start | bytes 9437184 | tf_op jit(solution)/shard_map/reduce_scatter | solution.py:66
  147.7 6.1 %copy-start.1 = (bf16[32,512,128]{1,2,0:T(8,128)(2,1)S(1)}, bf16[32,512,128]{1,2,0:T(8,128)(2,1)}, u32[]{:S(2)}) copy-start(bf16[32,512,128]{1,2,0:T(8,128)(2,1)} %copy-done) | copy-start | bytes 12582916
  159.6 374.6 %reduce-scatter.8.cloned.1.call-start = ((), (), s32[]{:S(2)}) async-start(), calls=%async_computation.7 | async-start | bytes 9437184 | tf_op jit(solution)/shard_map/reduce_scatter | solution.py:67
Sparse Core Ops, SparseCore 0:
  9.7 119.7 all-gather.1
  147.8 190.0 reduce-scatter.3
  341.0 96.5 reduce-scatter.5
  440.6 93.5 reduce-scatter.7
